TPU v7x, 32 devices: a whole 2x2x4 slice. The times are simulated.
32 devices in a mesh: prow: 4 (over x, core), pcol: 8 (over z, y).
Axes of the slice: x: 2, y: 2, z: 4, core: 2. Of those that a mesh axis runs over, the one named last changes fastest.
Arguments:
- child_u: bfloat16 [2, 10, 4, 2, 8, 512, 128], P(None, None, 'prow', None, 'pcol'), may hold values from -5 to 5
- child_v: bfloat16 [2, 10, 4, 2, 8, 512, 128], P(None, None, 'prow', None, 'pcol'), may hold values from -5 to 5
- child_rank: int32 [2, 10, 4, 2, 8], P(None, None, 'prow', None, 'pcol'), may hold values from 0 to 128, as said below
- diag_shift: float32 [16, 512], replicated, may hold values from 0.5 to 4
Outputs:
- front_out: float32 [10, 4, 512, 2, 8, 512], P(None, 'prow', None, None, 'pcol')
Inputs may be any that keep to these rules, and one draw needn't show every extreme that they name: `child_rank`: 0 on and above the block diagonal (i <= j); below it 0 where the child has no tile, else from 16 to 128.
All inputs are finite; a program needn't handle non-finite values.
Results may differ from a plain program's by a relative error of at most 0.0003.
Values may be sent and summed in bfloat16 or wider, within the bound.
A program may use at most 320 MiB of HBM per device.

v0:
```python
import jax
import jax.numpy as jnp
from jax import lax
from jax.sharding import PartitionSpec as P

PANELS = 2


def spread(value, axis, root):
    mine = lax.axis_index(axis) == root
    return lax.psum(jnp.where(mine, value, jnp.zeros_like(value)), axis)


def factor_panel(column, panel_index, block_rows, block_cols, own_column, prow_count, pcol_count):
    extent = column.shape[-1]
    pivot_tile = spread(column[panel_index // prow_count], "prow", panel_index % prow_count)
    is_owner = own_column == panel_index % pcol_count
    pivot_tile = jnp.where(is_owner, pivot_tile, jnp.eye(extent, dtype=jnp.float32))
    factor = jnp.linalg.cholesky(pivot_tile)
    solved = lax.linalg.triangular_solve(
        factor, column.reshape(-1, extent), left_side=False, lower=True, transpose_a=True
    ).reshape(column.shape)
    below_mask = (block_rows > panel_index)[:, None, None]
    solved = jnp.where(below_mask, solved, 0.0)
    pivot_diag = jnp.diagonal(factor)
    at_pivot = (block_rows == panel_index)[:, None, None]
    panel_out = jnp.where(
        at_pivot, (factor * pivot_diag[None, :])[None], solved * pivot_diag[None, None, :]
    )
    rounded = solved.astype(jnp.bfloat16)
    received = spread(rounded, "pcol", panel_index % pcol_count)
    picked = jnp.take(received, block_cols // prow_count, axis=0)
    column_rows = spread(picked, "prow", own_column % prow_count)
    return (received, column_rows, panel_out, is_owner)


def trailing(column, received, other_rows):
    return column - jnp.einsum(
        "rab,cb->rac", received, other_rows, preferred_element_type=jnp.float32
    )


def on_device(child_u, child_v, child_rank, diag_shift):
    prow_count = lax.axis_size("prow")
    pcol_count = lax.axis_size("pcol")
    own_row = lax.axis_index("prow")
    own_column = lax.axis_index("pcol")
    rank_grid = child_rank[:, :, 0, :, 0]
    rows_here = rank_grid.shape[1]
    cols_here = rank_grid.shape[2]
    extent = child_u.shape[-2]
    keep_mask = (
        jnp.arange(child_u.shape[-1], dtype=jnp.int32)[None, None, None, :]
        < rank_grid[:, :, :, None]
    ).astype(jnp.bfloat16)
    left_factor = child_u[:, :, 0, :, 0] * keep_mask[:, :, :, None, :]
    right_factor = child_v[:, :, 0, :, 0] * keep_mask[:, :, :, None, :]
    tile_grid = jnp.einsum(
        "crtak,crtbk->rtab", left_factor, right_factor, preferred_element_type=jnp.float32
    )
    row_terms = jnp.einsum(
        "crtak,crtbk->rab", left_factor, left_factor, preferred_element_type=jnp.float32
    )
    column_terms = jnp.einsum(
        "crtak,crtbk->tab", right_factor, right_factor, preferred_element_type=jnp.float32
    )
    kept_rows = cols_here * pcol_count // prow_count
    partial_rows = lax.psum(row_terms[:kept_rows], "pcol")
    spare_rows = jnp.zeros((rows_here - kept_rows, extent, extent), jnp.float32)
    row_sums = jnp.concatenate([partial_rows, spare_rows], axis=0)
    column_sums = lax.psum(column_terms, "prow")
    block_rows = jnp.arange(rows_here, dtype=jnp.int32) * prow_count + own_row
    block_cols = jnp.arange(cols_here, dtype=jnp.int32) * pcol_count + own_column
    slab_total = diag_shift.shape[0]
    select_cols = (block_cols[:, None] == jnp.arange(slab_total, dtype=jnp.int32)[None, :]).astype(
        jnp.float32
    )
    shift_cols = jnp.dot(select_cols, diag_shift, precision=lax.Precision.HIGHEST)
    identity = jnp.eye(extent, dtype=jnp.float32)
    diag_terms = (
        row_sums[:, None]
        + column_sums[None, :]
        + identity[None, None] * shift_cols[None, :, None, :]
    )
    on_diagonal = (block_rows[:, None] == block_cols[None, :])[:, :, None, None]
    tile_grid = tile_grid + jnp.where(on_diagonal, diag_terms, 0.0)
    columns = [tile_grid[:, column_index] for column_index in range(cols_here)]
    results = [jnp.zeros_like(columns[0]) for column_index in range(cols_here)]
    for panel_index in range(PANELS):
        local_col = panel_index // pcol_count
        received, column_rows, panel_out, is_owner = factor_panel(
            columns[local_col],
            panel_index,
            block_rows,
            block_cols,
            own_column,
            prow_count,
            pcol_count,
        )
        results[local_col] = jnp.where(is_owner, panel_out, results[local_col])
        columns = [
            trailing(columns[column_index], received, column_rows[column_index])
            for column_index in range(cols_here)
        ]
    outputs = []
    for column_index in range(cols_here):
        lower_mask = (block_rows >= block_cols[column_index])[:, None, None]
        finished = jnp.where(lower_mask, columns[column_index], 0.0)
        outputs.append(
            jnp.where(block_cols[column_index] < PANELS, results[column_index], finished)
        )
    stacked = jnp.stack(outputs, axis=1)
    return stacked.transpose(0, 2, 1, 3)[:, None, :, :, None, :]


def solution(mesh):
    placed = (
        P(None, None, "prow", None, "pcol", None, None),
        P(None, None, "prow", None, "pcol", None, None),
        P(None, None, "prow", None, "pcol"),
        P(),
    )
    return jax.shard_map(
        on_device,
        mesh=mesh,
        in_specs=placed,
        out_specs=P(None, "prow", None, None, "pcol", None),
        check_vma=False,
    )
```

profile of v0, /device:TPU:0, one launch (start us, length us, event | category | flops | bytes accessed | tf_op | source)
XLA Modules:
  0.0 1351.2 jit_solution(12334410048220816827)
XLA Ops:
  7.4 8.7 bitcast_multiply_fusion.1
  16.1 8.3 convolution_bitcast_fusion.2
  36.5 14.6 %convolution_bitcast_fusion = f32[10,2,512,512]{2,3,0,1:T(8,128)} fusion(bf16[2,10,2,512,128]{4,3,2,1,0:T(8,128)(2,1)} %get-tuple-element.69, bf16[2,10,2,512,128]{4,3,2,1,0:T(8,128)(2,1)} %get-tuple-element.68), kind=kOutput, calls=%fused_computation.35 | convolution fusion | flops 2684354560 | bytes 31457280 | tf_op jit(solution)/shard_map/crtak,crtbk->rtab/dot_general | solution.py:58
  51.1 27.6 %all-reduce.13.cloned.1.call-done = f32[2,512,512]{2,1,0:T(8,128)} async-done(((f32[2,512,512]{2,1,0:T(8,128)}), f32[2,512,512]{2,1,0:T(8,128)}) %all-reduce.13.cloned.1.call-update) | async-done | bytes 2097168 | tf_op jit(solution)/shard_map/psum | solution.py:71
  81.6 157.3 %all-reduce.11.cloned.1.call-done = f32[4,512,512]{2,1,0:T(8,128)} async-done(((f32[4,512,512]{2,1,0:T(8,128)}), f32[4,512,512]{2,1,0:T(8,128)}) %all-reduce.11.cloned.1.call-update) | async-done | bytes 4194320 | tf_op jit(solution)/shard_map/psum | solution.py:68
  251.6 12.6 copy_add_fusion
  273.0 9.1 slice_bitcast_fusion.1
  282.1 11.7 copy.45
  293.7 14.7 %all-reduce.15.cloned.1.call-done = f32[512,512]{0,1:T(8,128)} async-done(((f32[512,512]{0,1:T(8,128)}), f32[512,512]{0,1:T(8,128)}) %all-reduce.15.cloned.1.call-update) | async-done | bytes 1048592 | tf_op jit(solution)/shard_map/psum | solution.py:11
  311.6 11.7 cholesky.286
  323.3 9.8 custom-call.31
  333.9 11.7 cholesky.305
  345.7 10.0 custom-call.32
  356.3 11.7 cholesky.326
  368.8 9.8 custom-call.33
  379.2 11.7 cholesky.343
  397.9 11.7 while.4
  409.7 39.9 %custom-call.34 = f32[4,128,128]{1,2,0:T(8,128)} custom-call(f32[4,128,128]{2,1,0:T(8,128)S(1)} %get-tuple-element.22), custom_call_target="InvertDiagBlocksLowerTriangular" | custom-call | tf_op jit(solution)/shard_map/triangular_solve/custom-call.3 | solution.py:20
  462.9 10.0 convolution_subtract_fusion.1
  475.4 14.6 %fusion.20 = f32[5120,128]{1,0:T(8,128)S(1)} fusion(f32[5120,128]{0,1:T(8,128)S(1)} %fusion.71, f32[5120,128]{0,1:T(8,128)S(1)} %fusion.72, f32[5120,128]{0,1:T(8,128)S(1)} %bitcast.181, f32[5120,512]{1,0:T(8,128)S(1)} %bitcast.191, f32[512,512]{1,0:T(8,128)} %get-tuple-element.198), kind=kOutput, calls=%fused_computation.41 | convolution fusion | flops 3024486400 | bytes 13303808 | tf_op jit(solution)/shard_map/triangular_solve/dot.12 | solution.py:20
  497.1 11.4 copy.46
  508.5 11.3 copy.47
  519.7 7.9 fusion.23
  527.8 181.8 %all-reduce.17.cloned.1.call-done = bf16[10,512,512]{1,2,0:T(8,128)(2,1)} async-done(((bf16[10,512,512]{1,2,0:T(8,128)(2,1)}), bf16[10,512,512]{1,2,0:T(8,128)(2,1)}) %all-reduce.17.cloned.1.call-update) | async-done | bytes 5242896 | tf_op jit(solution)/shard_map/psum | solution.py:11
  714.1 35.4 %all-reduce.19.cloned.1.call-done = bf16[2,512,512]{1,2,0:T(8,128)(2,1)} async-done(((bf16[2,512,512]{1,2,0:T(8,128)(2,1)}), bf16[2,512,512]{1,2,0:T(8,128)(2,1)}) %all-reduce.19.cloned.1.call-update) | async-done | bytes 1048592 | tf_op jit(solution)/shard_map/psum | solution.py:11
  749.4 9.9 bitcast_subtract_fusion
  764.4 11.4 copy.53
  775.8 25.4 %all-reduce.21.cloned.1.call-done = f32[512,512]{0,1:T(8,128)} async-done(((f32[512,512]{0,1:T(8,128)}), f32[512,512]{0,1:T(8,128)}) %all-reduce.21.cloned.1.call-update) | async-done | bytes 1048592 | tf_op jit(solution)/shard_map/psum | solution.py:11
  802.9 11.7 cholesky.358
  814.8 9.8 custom-call.35
  827.2 11.7 cholesky.377
  840.3 10.2 custom-call.36
  852.0 11.7 cholesky.398
  864.4 9.8 custom-call.37
  875.7 11.7 cholesky.415
  894.0 11.8 while.5
  905.8 39.9 %custom-call.38 = f32[4,128,128]{1,2,0:T(8,128)} custom-call(f32[4,128,128]{2,1,0:T(8,128)S(1)} %get-tuple-element.23), custom_call_target="InvertDiagBlocksLowerTriangular" | custom-call | tf_op jit(solution)/shard_map/triangular_solve/custom-call.3 | solution.py:20
  959.0 10.2 convolution_subtract_fusion
  971.8 14.4 %fusion.17 = f32[5120,128]{1,0:T(8,128)S(1)} fusion(f32[5120,128]{0,1:T(8,128)S(1)} %fusion.65, f32[5120,128]{0,1:T(8,128)S(1)} %fusion.66, f32[5120,128]{0,1:T(8,128)S(1)} %bitcast.184, f32[5120,512]{1,0:T(8,128)S(1)} %bitcast.197, f32[512,512]{1,0:T(8,128)} %get-tuple-element.197), kind=kOutput, calls=%fused_computation.40 | convolution fusion | flops 3024486400 | bytes 13303808 | tf_op jit(solution)/shard_map/triangular_solve/dot.12 | solution.py:20
  993.2 11.4 copy.54
  1004.6 11.5 copy.55
  1032.1 176.3 %all-reduce.23.cloned.1.call-done = bf16[10,512,512]{1,2,0:T(8,128)(2,1)} async-done(((bf16[10,512,512]{1,2,0:T(8,128)(2,1)}), bf16[10,512,512]{1,2,0:T(8,128)(2,1)}) %all-reduce.23.cloned.1.call-update) | async-done | bytes 5242896 | tf_op jit(solution)/shard_map/psum | solution.py:11
  1212.6 8.3 fusion.47
  1226.0 22.1 %all-reduce.25.cloned.1.call-done = bf16[2,512,512]{1,2,0:T(8,128)(2,1)} async-done(((bf16[2,512,512]{1,2,0:T(8,128)(2,1)}), bf16[2,512,512]{1,2,0:T(8,128)(2,1)}) %all-reduce.25.cloned.1.call-update) | async-done | bytes 1048592 | tf_op jit(solution)/shard_map/psum | solution.py:11
  1248.0 18.4 %fusion.4 = f32[10,1,512,512]{2,3,0,1:T(8,128)} fusion(f32[10,512,512]{1,2,0:T(8,128)} %fusion.47, f32[10,2,512,512]{2,3,1,0:T(8,128)} %copy-done.2, pred[10]{0:T(512)(128)(4,1)S(1)} %get-tuple-element.76, pred[]{:T(512)S(6)} %lt.48, bf16[10,512,512]{1,2,0:T(8,128)(2,1)} %all-reduce.23.cloned.1.call-done, bf16[2,512,512]{1,2,0:T(8,128)(2,1)} %all-reduce.25.cloned.1.call-done), kind=kOutput, calls=%fused_computation.15 | convolution fusion | flops 2694840320 | bytes 37224460 | tf_op jit(solution)/shard_map/rab,cb->rac/dot_general | solution.py:38
  1266.4 18.5 %select_bitcast_fusion = f32[10,1,512,512]{2,3,0,1:T(8,128)} fusion(f32[10,512,512]{1,2,0:T(8,128)} %copy-done.3, f32[10,512,512]{1,2,0:T(8,128)} %copy.55, f32[10,512,512]{1,2,0:T(8,128)} %copy.47, f32[512]{0:T(512)S(1)} %gather_fusion.1, f32[512,512]{0,1:T(8,128)S(1)} %copy.56, f32[512]{0:T(512)S(1)} %gather_fusion, f32[512,512]{0,1:T(8,128)S(1)} %copy.52, ...), kind=kOutput, calls=%fused_computation.19 | convolution fusion | flops 2713190400 | bytes 49814020 | tf_op jit(solution)/shard_map/rab,cb->rac/dot_general | solution.py:38
  1284.9 16.2 %maximum_bitcast_fusion = f32[10,1,512,2,1,512]{2,5,0,3,4,1:T(8,128)} fusion(f32[10,1,512,512]{2,3,0,1:T(8,128)} %fusion.4, f32[10,1,512,512]{2,3,0,1:T(8,128)} %select_bitcast_fusion), kind=kLoop, calls=%fused_computation.8 | loop fusion | flops 5242880 | bytes 41943040 | tf_op jit(solution)/shard_map/broadcast_in_dim | solution.py:113
  1301.1 42.9 %copy.66 = f32[10,1,512,2,1,512]{5,4,3,2,1,0:T(1,128)} copy(f32[10,1,512,2,1,512]{2,5,0,3,4,1:T(8,128)} %maximum_bitcast_fusion) | data formatting | bytes 41943040 | tf_op jit(solution)/shard_map/broadcast_in_dim | solution.py:113
  (176 shorter events, 163.2 us)
Async XLA Ops:
  6.5 28.2 %copy-start = (f32[16,512]{1,0:T(8,128)S(1)}, f32[16,512]{1,0:T(8,128)}, u32[]{:S(2)}) copy-start(f32[16,512]{1,0:T(8,128)} %param.12) | copy-start | bytes 98308
  6.5 72.2 %all-reduce.13.cloned.1.call-start = ((), (), s32[]{:S(2)}) async-start(), calls=%async_computation.1 | async-start | bytes 4194304 | tf_op jit(solution)/shard_map/psum | solution.py:71
  24.5 214.4 %all-reduce.11.cloned.1.call-start = ((), (), s32[]{:S(2)}) async-start(), calls=%async_computation | async-start | bytes 8388608 | tf_op jit(solution)/shard_map/psum | solution.py:68
  33.4 275.0 %all-reduce.15.cloned.1.call-start = ((), (), s32[]{:S(2)}) async-start(), calls=%async_computation.2 | async-start | bytes 2097152 | tf_op jit(solution)/shard_map/psum | solution.py:11
  264.3 7.5 copy-start.2
  272.9 436.7 %all-reduce.17.cloned.1.call-start = ((), (), s32[]{:S(2)}) async-start(), calls=%async_computation.3 | async-start | bytes 10485760 | tf_op jit(solution)/shard_map/psum | solution.py:11
  310.1 87.8 %copy-start.13 = (s32[4]{0:T(128)S(1)}, s32[4]{0:T(128)}, u32[]{:S(2)}) copy-start(s32[4]{0:T(128)} %iota_multiply_fusion) | copy-start | bytes 52
  390.9 4.3 copy-start.6
  395.2 67.6 %slice-start = ((s8[10485760]{0:T(1024)(128)(4,1)}), s8[2097152]{0:T(1024)(128)(4,1)S(1)}, s32[]{:S(2)}) async-start(s8[10485760]{0:T(1024)(128)(4,1)} %bitcast.188), calls=%async_computation.8 | async-start | bytes 4194304
  449.6 13.3 slice-start.1
  454.0 6.3 copy-start.10
  454.0 8.9 slice-start.2
  508.5 11.3 copy-start.12
  527.7 221.7 %all-reduce.19.cloned.1.call-start = ((), (), s32[]{:S(2)}) async-start(), calls=%async_computation.4 | async-start | bytes 2097152 | tf_op jit(solution)/shard_map/psum | solution.py:11
  714.0 87.2 %all-reduce.21.cloned.1.call-start = ((), (), s32[]{:S(2)}) async-start(), calls=%async_computation.5 | async-start | bytes 2097152 | tf_op jit(solution)/shard_map/psum | solution.py:11
  759.3 3.8 copy-start.3
  764.3 444.1 %all-reduce.23.cloned.1.call-start = ((), (), s32[]{:S(2)}) async-start(), calls=%async_computation.6 | async-start | bytes 10485760 | tf_op jit(solution)/shard_map/psum | solution.py:11
  801.9 1.0 copy-start.7
  887.6 3.4 copy-start.5
  891.0 68.0 %slice-start.3 = ((s8[10485760]{0:T(1024)(128)(4,1)}), s8[2097152]{0:T(1024)(128)(4,1)S(1)}, s32[]{:S(2)}) async-start(s8[10485760]{0:T(1024)(128)(4,1)} %bitcast.194), calls=%async_computation.11 | async-start | bytes 4194304
  945.7 13.3 slice-start.4
  950.1 6.3 copy-start.11
  950.1 8.9 slice-start.5
  1024.0 224.1 %all-reduce.25.cloned.1.call-start = ((), (), s32[]{:S(2)}) async-start(), calls=%async_computation.7 | async-start | bytes 2097152 | tf_op jit(solution)/shard_map/psum | solution.py:11
  1031.6 181.0 %copy-start.8 = (bf16[2,512,512]{1,2,0:T(8,128)(2,1)S(1)}, bf16[2,512,512]{1,2,0:T(8,128)(2,1)}, u32[]{:S(2)}) copy-start(bf16[2,512,512]{1,2,0:T(8,128)(2,1)} %all-reduce.19.cloned.1.call-done) | copy-start | bytes 3145732
  1212.6 8.4 copy-start.4
  1248.0 18.4 %copy-start.9 = (bf16[2,512,512]{1,2,0:T(8,128)(2,1)S(1)}, bf16[2,512,512]{1,2,0:T(8,128)(2,1)}, u32[]{:S(2)}) copy-start(bf16[2,512,512]{1,2,0:T(8,128)(2,1)} %all-reduce.25.cloned.1.call-done) | copy-start | bytes 3145732
  1301.0 42.9 %copy-start.1 = (f32[16,512]{1,0:T(8,128)S(1)}, f32[16,512]{1,0:T(8,128)}, u32[]{:S(2)}) copy-start(f32[16,512]{1,0:T(8,128)} %param.12) | copy-start | bytes 98308
Sparse Core Ops, SparseCore 0:
  24.6 54.0 all-reduce.12
  82.4 156.4 all-reduce.10
  273.1 35.2 all-reduce.14
  527.8 181.7 all-reduce.16
  714.1 35.2 all-reduce.18
  764.4 36.7 all-reduce.20
  1024.1 184.2 all-reduce.22
  1212.7 35.2 all-reduce.24
where the time goes:
time: 1360 us; the launch traced here: 1350 us
  waiting for transfers between devices  641 us (47%)
  other arithmetic  318 us (23%)
  local copies, waits for them, and re-layouts  193 us (14%)
  matrix products  178 us (13%)
  between operations  21.1 us (2%)
    psum x6, waiting for transfers between devices, spread(): return lax.psum(jnp.where(mine, value, jnp.zeros_like(value)), axis)  456 us
    another operation x29, other arithmetic, factor_panel(): factor = jnp.linalg.cholesky(pivot_tile)  159 us
    psum x1, waiting for transfers between devices, on_device(): partial_rows = lax.psum(row_terms[:kept_rows], 'pcol')  157 us
    another operation x7, other arithmetic, factor_panel(): lax.linalg.triangular_solve(factor, column.reshape(-1, extent), left_side...  94.9 us
    another operation x14, matrix products, factor_panel(): lax.linalg.triangular_solve(factor, column.reshape(-1, extent), left_side...  85.9 us
    dot_general x4, matrix products, trailing(): jnp.einsum('rab,cb->rac', received, other_rows, preferred_element_type=jn...  55.1 us
    another operation x29, local copies, waits for them, and re-layouts, factor_panel(): lax.linalg.triangular_solve(factor, column.reshape(-1, extent), left_side...  46.2 us
    broadcast_in_dim x1, local copies, waits for them, and re-layouts, on_device(): return stacked.transpose(0, 2, 1, 3)[:, None, :, :, None, :]  42.9 us
  transfers between devices with their start and end apart: 8, of which 8 were waited for; matrix products, arithmetic and copies ran while one was open for 6% of the time, Pallas kernels for 0%

commit v1 on v0

v1 whole, which is shorter than its diff:
```python
import functools

import jax
import jax.numpy as jnp
from jax import lax
from jax.experimental import pallas as pl
from jax.experimental.pallas import tpu as pltpu
from jax.sharding import PartitionSpec as P

PANELS = 2
STEP = 128
SUB = 8


def nt(a, b, precision=None):
    return lax.dot_general(
        a, b, (((1,), (1,)), ((), ())), preferred_element_type=jnp.float32, precision=precision
    )


def nn(a, b, precision=None):
    return lax.dot_general(
        a, b, (((1,), (0,)), ((), ())), preferred_element_type=jnp.float32, precision=precision
    )


def factor_kernel(s_ref, c_ref, y_ref, w_ref, e_ref):
    extent = s_ref.shape[0]
    exact = lax.Precision.HIGHEST
    w_ref[...] = s_ref[...]
    e_ref[...] = (
        lax.broadcasted_iota(jnp.int32, (extent, extent), 0)
        == lax.broadcasted_iota(jnp.int32, (extent, extent), 1)
    ).astype(jnp.float32)
    groups = STEP // SUB
    sub_row = lax.broadcasted_iota(jnp.int32, (SUB, STEP), 0)
    lane = lax.broadcasted_iota(jnp.int32, (SUB, STEP), 1)

    @pl.loop(0, extent // STEP)
    def _(block):
        base = pl.multiple_of(block * STEP, STEP)
        here = pl.ds(base, STEP)
        tile = w_ref[here, here]
        left = [tile[g * SUB : (g + 1) * SUB] for g in range(groups)]
        right = [(lane == sub_row + g * SUB).astype(jnp.float32) for g in range(groups)]
        for j in range(STEP):
            own, inner = divmod(j, SUB)
            row = left[own][inner : inner + 1]
            inverse = 1.0 / jnp.broadcast_to(row[:, j : j + 1], (1, STEP))
            row_left = jnp.broadcast_to(row * inverse, (SUB, STEP))
            row_right = jnp.broadcast_to(right[own][inner : inner + 1] * inverse, (SUB, STEP))
            for g in range(own, groups):
                weight = jnp.broadcast_to(left[g][:, j : j + 1], (SUB, STEP))
                if g == own:
                    weight = jnp.where(sub_row > inner, weight, 0.0)
                left[g] = left[g] - weight * row_left
                right[g] = right[g] - weight * row_right
        upper = jnp.concatenate(left, axis=0)
        lower_inverse = jnp.concatenate(right, axis=0)
        tile_row = lax.broadcasted_iota(jnp.int32, (STEP, STEP), 0)
        tile_col = lax.broadcasted_iota(jnp.int32, (STEP, STEP), 1)
        pivots = jnp.sum(jnp.where(tile_row == tile_col, upper, 0.0), axis=1, keepdims=True)
        root = jnp.sqrt(pivots)
        pivot_factor = (jnp.where(tile_row <= tile_col, upper, 0.0) / root).T
        pivot_inverse = lower_inverse / root
        panel = nt(w_ref[:, here], pivot_inverse, exact)
        below = lax.broadcasted_iota(jnp.int32, (extent, STEP), 0) >= base + STEP
        panel = jnp.where(below, panel, 0.0)
        c_ref[:, here] = panel
        c_ref[here, here] = pivot_factor
        solved = nn(pivot_inverse, e_ref[here, :], exact)
        y_ref[here, :] = solved
        w_ref[...] -= nt(panel, panel, exact)
        e_ref[...] -= nn(panel, solved, exact)


def factor(pivot_tile):
    shape = jax.ShapeDtypeStruct(pivot_tile.shape, jnp.float32)
    spec = pl.BlockSpec(memory_space=pltpu.VMEM)
    return pl.pallas_call(
        factor_kernel,
        out_shape=(shape, shape),
        in_specs=[spec],
        out_specs=(spec, spec),
        scratch_shapes=[pltpu.VMEM(pivot_tile.shape, jnp.float32)] * 2,
        compiler_params=pltpu.CompilerParams(vmem_limit_bytes=24 * 2**20),
        cost_estimate=pl.CostEstimate(
            flops=60_000_000_000, bytes_accessed=3 * 2**20, transcendentals=0
        ),
        name="factor",
    )(pivot_tile)


def finish_kernel(prow_count, pcol_count, at_ref, u_ref, v_ref, g_ref, h_ref, d_ref, p_ref, o_ref):
    t, r = pl.program_id(0), pl.program_id(1)
    i = r * prow_count + at_ref[0]
    j = t * pcol_count + at_ref[1]

    @pl.when(i < j)
    def _():
        o_ref[0] = jnp.zeros_like(o_ref[0])

    @pl.when((i >= j) & (j < PANELS))
    def _():
        o_ref[0] = p_ref[0]

    @pl.when((i >= j) & (j >= PANELS))
    def _():
        total = -nt(g_ref[0], h_ref[0])
        for c in range(u_ref.shape[0]):
            total += nt(u_ref[c, 0, 0], v_ref[c, 0, 0])
        o_ref[0] = total

    @pl.when((i == j) & (j >= PANELS))
    def _():
        o_ref[0] += d_ref[0]


def finish(prow_count, pcol_count, at, left, right, solved, other, diag, panels):
    children, rows, cols, extent, rank = left.shape
    wide = solved.shape[-1]
    factor_spec = pl.BlockSpec((children, 1, 1, extent, rank), lambda t, r, at: (0, r, t, 0, 0))
    return pl.pallas_call(
        functools.partial(finish_kernel, prow_count, pcol_count),
        out_shape=jax.ShapeDtypeStruct((rows, extent, cols * extent), jnp.float32),
        grid_spec=pltpu.PrefetchScalarGridSpec(
            num_scalar_prefetch=1,
            grid=(cols, rows),
            in_specs=[
                factor_spec,
                factor_spec,
                pl.BlockSpec((1, extent, wide), lambda t, r, at: (r, 0, 0)),
                pl.BlockSpec((1, extent, wide), lambda t, r, at: (t, 0, 0)),
                pl.BlockSpec((1, extent, extent), lambda t, r, at: (t, 0, 0)),
                pl.BlockSpec(
                    (1, extent, extent), lambda t, r, at: (jnp.where(t == 0, r, rows - 1), 0, 0)
                ),
            ],
            out_specs=pl.BlockSpec((1, extent, extent), lambda t, r, at: (r, 0, t)),
        ),
        compiler_params=pltpu.CompilerParams(vmem_limit_bytes=48 * 2**20),
        cost_estimate=pl.CostEstimate(
            flops=2 * rows * cols * extent * extent * (wide + children * rank),
            bytes_accessed=60 * 2**20,
            transcendentals=0,
        ),
        name="finish",
    )(at, left, right, solved, other, diag, panels)


def pieces(value, count):
    parts = []
    for _ in range(count):
        part = lax.reduce_precision(value, 8, 7)
        parts.append(part.astype(jnp.bfloat16))
        value = value - part
    return parts


def times(left_parts, right_parts, pattern):
    total = None
    for a in left_parts:
        for b in right_parts:
            term = jnp.einsum(pattern, a, b, preferred_element_type=jnp.float32)
            total = term if total is None else total + term
    return total


def on_device(child_u, child_v, child_rank, diag_shift):
    prow_count = lax.axis_size("prow")
    pcol_count = lax.axis_size("pcol")
    own_row = lax.axis_index("prow")
    own_column = lax.axis_index("pcol")
    both = ("prow", "pcol")
    rank_grid = child_rank[:, :, 0, :, 0]
    rows_here = rank_grid.shape[1]
    cols_here = rank_grid.shape[2]
    extent = child_u.shape[-2]
    keep_mask = (
        jnp.arange(child_u.shape[-1], dtype=jnp.int32)[None, None, None, :]
        < rank_grid[:, :, :, None]
    ).astype(jnp.bfloat16)
    left = child_u[:, :, 0, :, 0] * keep_mask[:, :, :, None, :]
    right = child_v[:, :, 0, :, 0] * keep_mask[:, :, :, None, :]
    kept_rows = cols_here * pcol_count // prow_count
    row_terms = jnp.einsum(
        "crtak,crtbk->rab", left[:, :kept_rows], left[:, :kept_rows],
        preferred_element_type=jnp.float32,
    )
    column_terms = [
        jnp.einsum(
            "crak,crbk->ab", right[:, :, t], right[:, :, t], preferred_element_type=jnp.float32
        )
        for t in range(cols_here)
    ]
    zero = jnp.zeros((extent, extent), jnp.float32)
    pivot_parts = []
    for k in range(PANELS):
        row, col = k // prow_count, k // pcol_count
        in_row = own_row == k % prow_count
        in_col = own_column == k % pcol_count
        part = jnp.where(in_col, column_terms[col], zero)
        part = part + jnp.where(in_row, row_terms[row], zero)
        own_tile = jnp.einsum(
            "cak,cbk->ab", left[:, row, col], right[:, row, col],
            preferred_element_type=jnp.float32,
        )
        pivot_parts.append(part + jnp.where(in_row & in_col, own_tile, zero))
    pivot_sums = lax.psum(jnp.stack(pivot_parts), both)

    pairs = [(m, k) for k in range(PANELS) for m in range(k + 1, PANELS)]
    pair_factors = []
    for m, k in pairs:
        root = (own_row == m % prow_count) & (own_column == k % pcol_count)
        tile = jnp.stack(
            [f[:, m // prow_count, k // pcol_count] for f in (left, right)]
        )
        pair_factors.append(jnp.where(root, tile, jnp.zeros_like(tile)))
    pair_factors = lax.psum(jnp.stack(pair_factors), both)

    panel_factors = []
    for k in range(PANELS):
        tiles = jnp.stack([f[:, :, k // pcol_count] for f in (left, right)])
        panel_factors.append(
            jnp.where(own_column == k % pcol_count, tiles, jnp.zeros_like(tiles))
        )
    panel_factors = lax.psum(jnp.stack(panel_factors), "pcol")

    block_rows = jnp.arange(rows_here, dtype=jnp.int32) * prow_count + own_row
    block_cols = jnp.arange(cols_here, dtype=jnp.int32) * pcol_count + own_column
    other_factors = jnp.take(panel_factors, block_cols // prow_count, axis=3)
    other_factors = lax.psum(
        jnp.where(own_row == own_column % prow_count, other_factors, jnp.zeros_like(other_factors)),
        "prow",
    )
    row_sums = lax.psum(row_terms, "pcol")
    column_sums = lax.psum(jnp.stack(column_terms), "prow")

    identity = jnp.eye(extent, dtype=jnp.float32)
    near_rows = jnp.concatenate([block_rows, block_cols])
    near_factors = jnp.concatenate([panel_factors, other_factors], axis=3)
    rounded = []
    fixed = {m: [] for m in range(PANELS)}
    panels = jnp.zeros((rows_here, extent, extent), jnp.float32)
    for k in range(PANELS):
        pivot_tile = pivot_sums[k] + identity * diag_shift[k][None, :]
        for g in fixed[k]:
            pivot_tile = pivot_tile - nt(g, g)
        lower, inverse = factor(pivot_tile)
        inverse_parts = pieces(inverse, 3)
        carried = [pieces(times(inverse_parts, [g], "ab,bk->ak"), 2) for g in fixed[k]]

        def solve(left_tiles, right_tiles, earlier):
            moved = times(inverse_parts, [right_tiles], "ab,crbk->crak")
            value = times([left_tiles], pieces(moved, 2), "crak,crbk->rab")
            for g, parts in zip(earlier, carried):
                value = value - times([g], parts, "rak,bk->rab")
            return value

        for position, (m, kk) in enumerate(pairs):
            if kk == k:
                tile = pair_factors[position]
                earlier = [g[None] for g in fixed[m]]
                value = solve(tile[0][:, None], tile[1][:, None], earlier)
                fixed[m].append(value[0].astype(jnp.bfloat16))
        value = solve(near_factors[k, 0], near_factors[k, 1], rounded)
        value = jnp.where((near_rows > k)[:, None, None], value, 0.0)
        rounded.append(value.astype(jnp.bfloat16))
        scale = jnp.diagonal(lower)
        panel = jnp.where(
            (block_rows == k)[:, None, None], lower[None], value[:rows_here]
        ) * scale[None, None, :]
        panels = jnp.where(own_column == k % pcol_count, panel, panels)

    wide = jnp.concatenate(rounded, axis=-1)
    select_cols = (
        block_cols[:, None] == jnp.arange(diag_shift.shape[0], dtype=jnp.int32)[None, :]
    ).astype(jnp.float32)
    shift_cols = jnp.dot(select_cols, diag_shift, precision=lax.Precision.HIGHEST)
    diag = (
        jnp.take(row_sums, block_cols // prow_count, axis=0)
        + column_sums
        + identity[None] * shift_cols[:, None, :]
    )
    at = jnp.stack([own_row, own_column]).astype(jnp.int32)
    out = finish(
        prow_count, pcol_count, at, left, right, wide[:rows_here], wide[rows_here:], diag, panels
    )
    return out.reshape(rows_here, 1, extent, cols_here, 1, extent)


def solution(mesh):
    placed = (
        P(None, None, "prow", None, "pcol", None, None),
        P(None, None, "prow", None, "pcol", None, None),
        P(None, None, "prow", None, "pcol"),
        P(),
    )
    return jax.shard_map(
        on_device,
        mesh=mesh,
        in_specs=placed,
        out_specs=P(None, "prow", None, None, "pcol", None),
        check_vma=False,
    )
```

time: 1360 us -> 1080 us (0.79)
  other arithmetic: 318 us -> 54.6 us
  Pallas kernels: 0 us -> 135 us
  local copies, waits for them, and re-layouts: 193 us -> 103 us
  matrix products: 178 us -> 106 us
  waiting for transfers between devices: 641 us -> 661 us
    another operation x36 -> x4, other arithmetic: 254 us -> 12.3 us  [the longest x1 9.22 us: on_device(): panel_factors = lax.psum(jnp.stack(panel_factors), 'pcol')]
    pallas_call x0 -> x3, Pallas kernels: none -> 135 us  [the longest x2 106 us: factor(): pl.pallas_call(factor_kernel, out_shape=(shape, shape), in_specs=[spec],...]
    another operation x26 -> x0, matrix products: 93.2 us -> none  [the longest x14 85.9 us: factor_panel(): lax.linalg.triangular_solve(factor, column.reshape(-1, extent), left_side...]
    broadcast_in_dim x1 -> x0, local copies, waits for them, and re-layouts: 42.9 us -> none  [on_device(): return stacked.transpose(0, 2, 1, 3)[:, None, :, :, None, :]]
    another operation x37 -> x4, local copies, waits for them, and re-layouts: 46.5 us -> 5.95 us  [the longest x2 4 us: on_device(): tiles = jnp.stack([f[:, :, k // pcol_count] for f in (left, right)])]
    dot_general x7 -> x25, matrix products: 84.5 us -> 106 us  [the longest x20 95.1 us: times(): term = jnp.einsum(pattern, a, b, preferred_element_type=jnp.float32)]
    psum x8 -> x6, waiting for transfers between devices: 640 us -> 660 us  [the longest x1 269 us: on_device(): panel_factors = lax.psum(jnp.stack(panel_factors), 'pcol')]
    broadcast_in_dim x1 -> x0, other arithmetic: 16.2 us -> none  [on_device(): return stacked.transpose(0, 2, 1, 3)[:, None, :, :, None, :]]
  transfers between devices with their start and end apart: 8 -> 6, of which waited for: 8 -> 6; matrix products, arithmetic and copies ran while one was open for 6% -> 9% of each run, Pallas kernels for 0% -> 10%
where the time goes in v1:
time: 1080 us; the launch traced here: 1070 us
  waiting for transfers between devices  661 us (61%)
  Pallas kernels  135 us (12%)
  matrix products  106 us (10%)
  local copies, waits for them, and re-layouts  103 us (10%)
  other arithmetic  54.6 us (5%)
  between operations  14.1 us (1%)
    psum x1, waiting for transfers between devices, on_device(): panel_factors = lax.psum(jnp.stack(panel_factors), 'pcol')  269 us
    psum x1, waiting for transfers between devices, on_device(): row_sums = lax.psum(row_terms, 'pcol')  124 us
    pallas_call x2, Pallas kernels, factor(): pl.pallas_call(factor_kernel, out_shape=(shape, shape), in_specs=[spec],...  106 us
    psum x1, waiting for transfers between devices, on_device(): pivot_sums = lax.psum(jnp.stack(pivot_parts), both)  102 us
    dot_general x20, matrix products, times(): term = jnp.einsum(pattern, a, b, preferred_element_type=jnp.float32)  95.1 us
    psum x1, waiting for transfers between devices, on_device(): pair_factors = lax.psum(jnp.stack(pair_factors), both)  79.4 us
    psum x1, waiting for transfers between devices, on_device(): column_sums = lax.psum(jnp.stack(column_terms), 'prow')  48.4 us
    psum x1, waiting for transfers between devices, on_device(): lax.psum(jnp.where(own_row == own_column % prow_count, other_factors, jnp...  37.4 us
  transfers between devices with their start and end apart: 6, of which 6 were waited for; matrix products, arithmetic and copies ran while one was open for 9% of the time, Pallas kernels for 10%

profile of v1, /device:TPU:0, one launch (start us, length us, event | category | flops | bytes accessed | tf_op | source)
XLA Modules:
  0.0 1074.8 jit_solution(15455139120487339369)
XLA Ops:
  7.4 2.8 bitcast_multiply_fusion.v_ref
  10.3 1.5 fusion.19
  11.8 2.8 copy-done.11
  15.0 2.3 copy-done.8
  17.3 3.2 convolution_bitcast_fusion
  20.5 1.9 fusion.50
  26.9 2.0 copy_bitcast_fusion
  28.9 2.0 slice_bitcast_fusion.10
  30.9 4.3 broadcast_select_fusion.1
  35.2 9.2 pad_maximum_fusion
  45.1 4.1 fusion.34
  53.1 5.5 copy.67.u_ref
  59.6 101.9 %all-reduce.11.cloned.1.call-done = f32[2,512,512]{2,1,0:T(8,128)} async-done(((f32[2,512,512]{2,1,0:T(8,128)}), f32[2,512,512]{2,1,0:T(8,128)}) %all-reduce.11.cloned.1.call-update) | async-done | bytes 2097168 | tf_op jit(solution)/shard_map/psum | solution.py:209
  162.8 52.7 %factor.2 = (f32[512,512]{1,0:T(8,128)S(1)}, f32[512,512]{1,0:T(8,128)S(1)}) custom-call(f32[512,512]{1,0:T(8,128)S(1)} %fusion.45.s_ref), custom_call_target="tpu_custom_call" | custom-call | flops 60000002048 | bytes 3145728 | tf_op jit(solution)/shard_map/factor/pallas_call | solution.py:80
  215.5 79.4 %all-reduce.13.cloned.1.call-done = bf16[1,2,2,512,128]{4,3,2,1,0:T(8,128)(2,1)} async-done(((bf16[1,2,2,512,128]{4,3,2,1,0:T(8,128)(2,1)}), bf16[1,2,2,512,128]{4,3,2,1,0:T(8,128)(2,1)}) %all-reduce.13.cloned.1.call-update) | async-done | bytes 524304 | tf_op jit(solution)/shard_map/psum | solution.py:219
  300.2 52.8 %factor.3 = (f32[512,512]{1,0:T(8,128)S(1)}, f32[512,512]{1,0:T(8,128)S(1)}) custom-call(f32[512,512]{1,0:T(8,128)S(1)} %convolution_subtract_fusion.s_ref), custom_call_target="tpu_custom_call" | custom-call | flops 60000002048 | bytes 3145728 | tf_op jit(solution)/shard_map/factor/pallas_call | solution.py:80
  355.9 269.0 %all-reduce.7.cloned.1.call-done = bf16[2,2,2,10,512,128]{5,4,2,3,1,0:T(8,128)(2,1)} async-done(((bf16[2,2,2,10,512,128]{5,4,2,3,1,0:T(8,128)(2,1)}), bf16[2,2,2,10,512,128]{5,4,2,3,1,0:T(8,128)(2,1)}) %all-reduce.7.cloned.1.call-update) | async-done | bytes 10485776 | tf_op jit(solution)/shard_map/psum | solution.py:227
  624.9 9.7 copy.40
  634.6 6.1 gather_fusion
  640.7 3.3 fusion.33
  644.0 2.8 convolution_add_fusion
  646.9 4.5 gather_fusion.3
  651.4 8.6 gather_fusion.2
  660.0 123.8 %all-reduce.15.cloned.1.call-done = f32[4,512,512]{2,1,0:T(8,128)} async-done(((f32[4,512,512]{2,1,0:T(8,128)}), f32[4,512,512]{2,1,0:T(8,128)}) %all-reduce.15.cloned.1.call-update) | async-done | bytes 4194320 | tf_op jit(solution)/shard_map/psum | solution.py:236
  783.8 4.2 gather_fusion.1
  788.0 48.4 %all-reduce.17.cloned.1.call-done = f32[2,512,512]{2,1,0:T(8,128)} async-done(((f32[2,512,512]{2,1,0:T(8,128)}), f32[2,512,512]{2,1,0:T(8,128)}) %all-reduce.17.cloned.1.call-update) | async-done | bytes 2097168 | tf_op jit(solution)/shard_map/psum | solution.py:237
  836.5 4.5 multiply_add_fusion.d_ref
  841.0 11.8 %constant_dynamic-update-slice_fusion.1 = bf16[2,2,2,12,512,128]{5,4,2,3,1,0:T(8,128)(2,1)} fusion(bf16[2,2,2,10,512,128]{5,4,2,3,1,0:T(8,128)(2,1)} %all-reduce.7.cloned.1.call-done), kind=kLoop, calls=%fused_computation.145 | loop fusion | bytes 20971520
  852.8 37.4 %all-reduce.9.cloned.1.call-done = bf16[2,2,2,2,512,128]{5,4,2,3,1,0:T(8,128)(2,1)} async-done(((bf16[2,2,2,2,512,128]{5,4,2,3,1,0:T(8,128)(2,1)}), bf16[2,2,2,2,512,128]{5,4,2,3,1,0:T(8,128)(2,1)}) %all-reduce.9.cloned.1.call-update) | async-done | bytes 2097168 | tf_op jit(solution)/shard_map/psum | solution.py:232
  890.2 3.4 constant_dynamic-update-slice_fusion
  893.5 3.3 slice_bitcast_fusion
  896.8 4.6 fusion.22
  901.4 4.6 fusion.24
  906.0 1.9 fusion.27
  907.8 1.9 fusion.29
  909.7 4.9 fusion.9
  914.6 7.5 fusion.16
  922.1 12.8 %fusion.91 = (bf16[12,512,512]{2,1,0:T(8,128)(2,1)S(1)}, f32[12,512,512]{2,1,0:T(8,128)}) fusion(bf16[2,12,512,128]{2,3,1,0:T(8,128)(2,1)} %get-tuple-element.17, bf16[2,2,2,12,512,128]{5,4,2,3,1,0:T(8,128)(2,1)} %constant_dynamic-update-slice_fusion, f32[12,512,512,1]{2,1,3,0:T(8,128)} %fusion.16, pred[12]{0:T(512)(128)(4,1)S(1)} %copy-done.15), kind=kOutput, calls=%fused_computation.177 | convolution fusion | flops 1620049920 | bytes 37748748 | tf_op jit(solution)/shard_map/crak,crbk->rab/dot_general | solution.py:164
  934.9 6.7 fusion.55
  942.3 6.5 fusion.58
  948.9 5.5 fusion.11
  954.4 7.6 fusion.13
  962.0 21.3 %fusion.92 = (bf16[12,512,512]{2,1,0:T(8,128)(2,1)}, f32[12,512,512]{2,1,0:T(8,128)}) fusion(f32[12,512,512]{2,1,0:T(8,128)} %fusion.58, f32[12,512,512]{2,1,0:T(8,128)} %fusion.55, bf16[2,12,512,128]{2,3,1,0:T(8,128)(2,1)S(1)} %get-tuple-element.15, bf16[2,2,2,12,512,128]{5,4,2,3,1,0:T(8,128)(2,1)} %constant_dynamic-update-slice_fusion, ...), kind=kOutput, calls=%fused_computation.178 | convolution fusion | flops 1626341376 | bytes 62914572 | tf_op jit(solution)/shard_map/crak,crbk->rab/dot_general | solution.py:164
  983.3 2.0 pad_maximum_fusion.2.h_ref
  986.8 9.9 fusion.3.g_ref
  996.7 10.5 fusion.6.p_ref
  1007.1 29.7 %finish.1 = f32[10,512,1024]{2,1,0:T(8,128)} custom-call(s32[2]{0:T(128)S(1)} %pad_add_fusion.at_ref, bf16[2,10,2,512,128]{4,3,2,1,0:T(8,128)(2,1)} %copy.67.u_ref, bf16[2,10,2,512,128]{4,3,2,1,0:T(8,128)(2,1)} %copy-done.7, bf16[10,512,1024]{2,1,0:T(8,128)(2,1)} %fusion.3.g_ref, bf16[2,512,1024]{2,1,0:T(8,128)(2,1)S(1)} %pad_maximum_fusion.2.h_ref, ...), custom_call_target="tpu_custom_call" | custom-call | flops 13421772800 | bytes 62914560 | tf_op jit(solution)/shard_map/finish/pallas_call | solution.py:123
  1036.9 30.9 %reshape.327 = f32[10,1,512,2,1,512]{5,4,3,2,1,0:T(1,128)} reshape(f32[10,512,1024]{2,1,0:T(8,128)} %finish.1) | data formatting | bytes 41943040 | tf_op jit(solution)/shard_map/reshape | solution.py:289
  (93 shorter events, 22.6 us)
Async XLA Ops:
  6.5 154.9 %all-reduce.11.cloned.1.call-start = ((), (), s32[]{:S(2)}) async-start(), calls=%async_computation.2 | async-start | bytes 4194304 | tf_op jit(solution)/shard_map/psum | solution.py:209
  10.3 4.7 copy-start.7
  10.3 4.4 copy-start.11
  15.0 2.3 copy-start.8
  23.9 271.0 %all-reduce.13.cloned.1.call-start = ((), (), s32[]{:S(2)}) async-start(), calls=%async_computation.3 | async-start | bytes 1048576 | tf_op jit(solution)/shard_map/psum | solution.py:219
  26.8 598.1 %all-reduce.7.cloned.1.call-start = ((), (), s32[]{:S(2)}) async-start(), calls=%async_computation | async-start | bytes 20971520 | tf_op jit(solution)/shard_map/psum | solution.py:227
  44.5 739.4 %all-reduce.15.cloned.1.call-start = ((), (), s32[]{:S(2)}) async-start(), calls=%async_computation.4 | async-start | bytes 8388608 | tf_op jit(solution)/shard_map/psum | solution.py:236
  45.0 791.4 %all-reduce.17.cloned.1.call-start = ((), (), s32[]{:S(2)}) async-start(), calls=%async_computation.5 | async-start | bytes 4194304 | tf_op jit(solution)/shard_map/psum | solution.py:237
  50.8 839.4 %all-reduce.9.cloned.1.call-start = ((), (), s32[]{:S(2)}) async-start(), calls=%async_computation.1 | async-start | bytes 4194304 | tf_op jit(solution)/shard_map/psum | solution.py:232
  53.1 5.5 copy-start.18
  294.9 4.1 copy-start.12
  294.9 4.8 copy-start.13
  299.7 54.7 %copy-start.9 = (bf16[512,512]{1,0:T(8,128)(2,1)}, bf16[512,512]{1,0:T(8,128)(2,1)S(1)}, u32[]{:S(2)}) copy-start(bf16[512,512]{1,0:T(8,128)(2,1)S(1)} %fusion.36) | copy-start | bytes 1572868
  353.0 1.0 copy-start
  896.8 4.6 copy-start.5
  914.6 7.5 copy-start.15
  922.1 12.8 %copy-start.10 = (f32[512,512]{1,0:T(8,128)S(1)}, f32[512,512]{1,0:T(8,128)}, u32[]{:S(2)}) copy-start(f32[512,512]{1,0:T(8,128)} %convolution_add_fusion) | copy-start | bytes 3145732
  934.9 7.4 copy-start.3
  934.9 13.9 %slice-start.3 = ((s8[6291456]{0:T(1024)(128)(4,1)}), s8[4194304]{0:T(1024)(128)(4,1)S(1)}, s32[]{:S(2)}) async-start(s8[6291456]{0:T(1024)(128)(4,1)} %bitcast.218), calls=%async_computation.9 | async-start | bytes 8388608
  942.3 6.6 copy-start.6
  942.3 6.6 slice-start.4
  954.4 7.6 copy-start.14
  983.3 3.4 copy-start.4
  983.3 13.3 %slice-start = ((s8[12582912]{0:T(1024)(128)(4,1)}), s8[4194304]{0:T(1024)(128)(4,1)S(1)}, s32[]{:S(2)}) async-start(s8[12582912]{0:T(1024)(128)(4,1)} %bitcast.216), calls=%async_computation.6 | async-start | bytes 8388608
  983.3 13.3 %slice-start.1 = ((s8[12582912]{0:T(1024)(128)(4,1)}), s8[4194304]{0:T(1024)(128)(4,1)S(1)}, s32[]{:S(2)}) async-start(s8[12582912]{0:T(1024)(128)(4,1)} %bitcast.216), calls=%async_computation.7 | async-start | bytes 8388608
  986.7 9.9 copy-start.1
  986.7 9.9 slice-start.2
  986.7 9.9 copy-start.16
  986.7 9.9 copy-start.17
  996.7 10.5 copy-start.2
Sparse Core Ops, SparseCore 0:
  24.0 137.3 all-reduce.10
  166.7 128.1 all-reduce.12
  298.8 326.0 all-reduce.6
  628.4 155.3 all-reduce.14
  786.1 50.3 all-reduce.16
  838.7 51.4 all-reduce.8
